TPU v7x, 32 devices: a whole 2x2x4 slice. The times are simulated.
32 devices in a mesh: table: 16 (over z, y, x), narrow: 2 (over core).
Axes of the slice: x: 2, y: 2, z: 4, core: 2. Of those that a mesh axis runs over, the one named last changes fastest.
Arguments:
- table_rows: bfloat16 [16384, 256], P('table'), may hold values from -3 to 3
- accum: float32 [16384], P('table'), may hold values from 1 to 100
- factor_down: bfloat16 [2048, 256], P('narrow'), may hold values from -0.125 to 0.125
- factor_up: bfloat16 [2048, 256], P('narrow'), may hold values from -0.375 to 0.375
- cross_bias: float32 [2048], replicated, may hold values from -3 to 3
- out_weight: bfloat16 [2048], replicated, may hold values from -0.125 to 0.125
- target: float32 [4096], P(('table', 'narrow')), may hold values from 0 to 1
- bag_rows: int32 [512, 512], P(('table', 'narrow')), may hold values from -1 to 1023, as said below
- slot_target: int32 [512, 128], P(('table', 'narrow')), may hold values from -1 to 1023, as said below
Outputs:
- logits: float32 [4096], P(('table', 'narrow'))
- down_grad: float32 [2048, 256], P('narrow')
- up_grad: float32 [2048, 256], P('narrow')
- new_rows: bfloat16 [16384, 256], P('table')
- new_accum: float32 [16384], P(('table', 'narrow'))
Inputs may be any that keep to these rules, and one draw needn't show every extreme that they name: `slot_target`: for each source device (its 16 rows): every bag 0 .. 1023 is named by exactly one slot and the other slots hold -1; in every draw each source device has one window all of whose 128 slots are used. `bag_rows`: A used slot holds 1 to 4 rows of the window first and -1 after them; an unused slot holds -1 only; each source device has a slot with 4 lookups.
All inputs are finite; a program needn't handle non-finite values.
Results may differ from a plain program's by a relative error of at most 0.0077.
Values may be sent and summed in bfloat16 or wider, within the bound.
No kernel may reach another device: no remote copies, remote signals or barrier semaphores. Data moves between devices by JAX's collectives and lax.ppermute only.
A program may use at most 64 MiB of HBM per device.

v0:
```python
import math
import jax
import jax.numpy as jnp
from jax import lax
from jax.sharding import PartitionSpec as P

FEAT = 8
HOT = 4
LEARN_RATE = 0.2
LOSS_SCALE = 32.0
ADA_EPS = 1e-06


def transposed_dot(left, right):
    return lax.dot_general(
        left, right, (((0,), (0,)), ((), ())), preferred_element_type=jnp.float32
    )


def rows_dot(left, right):
    return lax.dot_general(
        left, right, (((1,), (1,)), ((), ())), preferred_element_type=jnp.float32
    )


def local(
    table_rows, accum, factor_down, factor_up, cross_bias, out_weight, target, bag_rows, slot_target
):
    tables = lax.axis_size("table")
    narrows = lax.axis_size("narrow")
    row_dev, emb_width = table_rows.shape
    pools_per = slot_target.shape[1]
    samples = target.shape[0]
    bag_count = samples * FEAT
    slot_count = tables * pools_per
    asked = lax.all_to_all(bag_rows, "table", split_axis=0, concat_axis=0, tiled=True)
    lookup_ids = asked.reshape(slot_count, HOT)
    positions = lax.broadcasted_iota(jnp.int32, (1, row_dev), 1)
    counts = jnp.zeros((slot_count, row_dev), jnp.bfloat16)
    for lookup in range(HOT):
        counts = counts + (lookup_ids[:, lookup : lookup + 1] == positions).astype(jnp.bfloat16)
    pool_sums = jnp.dot(counts, table_rows, preferred_element_type=jnp.float32)
    pool_out = pool_sums.astype(jnp.bfloat16).reshape(tables, pools_per, emb_width)
    arrived = lax.all_to_all(pool_out, "table", split_axis=0, concat_axis=0, tiled=True).reshape(
        slot_count, emb_width
    )
    bag_index = lax.broadcasted_iota(jnp.int32, (bag_count, 1), 0)
    placing = (slot_target.reshape(1, slot_count) == bag_index).astype(jnp.bfloat16)
    pooled_feats = (
        jnp.dot(placing, arrived, preferred_element_type=jnp.float32)
        .astype(jnp.bfloat16)
        .reshape(samples, FEAT * emb_width)
    )
    down_full, up_full = (
        lax.all_gather(factor_down, "narrow", axis=0, tiled=True),
        lax.all_gather(factor_up, "narrow", axis=0, tiled=True),
    )
    hidden = jnp.dot(pooled_feats, down_full, preferred_element_type=jnp.float32).astype(
        jnp.bfloat16
    )
    cross_out = rows_dot(hidden, up_full)
    feats_f = pooled_feats.astype(jnp.float32)
    shifted = cross_out + cross_bias
    mixed_out = feats_f * shifted + feats_f
    weight_f = out_weight.astype(jnp.float32)
    logits = jnp.sum(mixed_out * weight_f, axis=1)
    dlogit = LOSS_SCALE * (jax.nn.sigmoid(logits) - target)
    dmixed = dlogit[:, None] * weight_f
    dcross = (dmixed * feats_f).astype(jnp.bfloat16)
    dhidden = jnp.dot(dcross, up_full, preferred_element_type=jnp.float32).astype(jnp.bfloat16)
    back_term = rows_dot(dhidden, down_full)
    dpooled = (dmixed * (shifted + 1.0) + back_term).astype(jnp.bfloat16)
    narrow_sum = lax.psum_scatter(
        jnp.concatenate(
            [transposed_dot(pooled_feats, dhidden), transposed_dot(dcross, hidden)], axis=1
        ).astype(jnp.bfloat16),
        "narrow",
        scatter_dimension=0,
        tiled=True,
    ).astype(jnp.float32)
    grand_total = lax.psum(narrow_sum, "table")
    batch_all = samples * tables * narrows
    grand_total = grand_total * (1.0 / math.sqrt(batch_all))
    rank_size = factor_down.shape[1]
    down_grad = grand_total[:, :rank_size]
    up_grad = grand_total[:, rank_size:]
    bag_grads = dpooled.reshape(bag_count, emb_width)
    slot_grads = (
        transposed_dot(placing, bag_grads)
        .astype(jnp.bfloat16)
        .reshape(tables, pools_per, emb_width)
    )
    returned = lax.all_to_all(slot_grads, "table", split_axis=0, concat_axis=0, tiled=True).reshape(
        slot_count, emb_width
    )
    local_grad = transposed_dot(counts, returned)
    narrow_index = lax.axis_index("narrow")
    share_size = row_dev // narrows
    row_grad = lax.psum(local_grad.astype(jnp.bfloat16), "narrow").astype(jnp.float32)
    accum_all = accum + jnp.mean(row_grad * row_grad, axis=1)
    new_rows = (
        table_rows.astype(jnp.float32)
        - LEARN_RATE * row_grad * lax.rsqrt(accum_all + ADA_EPS)[:, None]
    ).astype(jnp.bfloat16)
    new_accum = lax.dynamic_slice_in_dim(accum_all, narrow_index * share_size, share_size, 0)
    return (logits, down_grad, up_grad, new_rows, new_accum)


def solution(mesh):
    in_specs = (
        P("table", None),
        P("table"),
        P("narrow", None),
        P("narrow", None),
        P(),
        P(),
        P(("table", "narrow")),
        P(("table", "narrow"), None),
        P(("table", "narrow"), None),
    )
    out_specs = (
        P(("table", "narrow")),
        P("narrow", None),
        P("narrow", None),
        P("table", None),
        P(("table", "narrow")),
    )
    return jax.shard_map(local, mesh=mesh, in_specs=in_specs, out_specs=out_specs, check_vma=False)
```

profile of v0, /device:TPU:0, one launch (start us, length us, event | category | flops | bytes accessed | tf_op | source)
XLA Modules:
  0.0 247.3 jit_solution(3443778541291321474)
XLA Ops:
  7.2 0.8 all_to_all.12
  8.0 15.5 %all_to_all.19 = s32[16,1,512]{2,1,0:T(1,128)S(1)} all-to-all(s32[16,1,512]{2,1,0:T(1,128)S(1)} %all_to_all.12), channel_id=1, replica_groups=mesh['table'=16,'narrow'=2] {'table'}, dimensions={0} | all-to-all | bytes 65536 | tf_op jit(solution)/shard_map/all_to_all | solution.py:36
  23.5 1.1 reshape.40
  24.6 2.0 slice_reduce_fusion.3
  26.6 6.1 %fusion.15 = bf16[2048,256]{1,0:T(8,128)(2,1)} fusion(bf16[1024,256]{1,0:T(8,128)(2,1)S(1)} %copy-done.2, s32[2048]{0:T(1024)S(1)} %get-tuple-element.21, s32[2048]{0:T(1024)S(1)} %get-tuple-element.22, s32[2048]{0:T(1024)S(1)} %get-tuple-element.23, s32[2048]{0:T(1024)S(1)} %get-tuple-element.20), kind=kOutput, calls=%fused_computation.18 | convolution fusion | flops 1107820544 | bytes 1605632 | tf_op jit(solution)/shard_map/dot_general | solution.py:42
  32.7 3.8 %all-to-all-start.1 = ((bf16[16,128,256]{2,1,0:T(8,128)(2,1)}), bf16[16,128,256]{2,1,0:T(8,128)(2,1)S(1)}, u32[]{:S(2)}, u32[]{:S(2)}) async-start(bf16[16,128,256]{2,1,0:T(8,128)(2,1)} %bitcast.1), calls=%async_computation.1 | async-start | bytes 2097152 | tf_op jit(solution)/shard_map/all_to_all | solution.py:44
  36.5 0.7 all-gather.3.cloned.1.call-update
  37.3 0.7 all-gather.5.cloned.1.call-update
  38.0 21.7 %all-to-all-done.1 = bf16[16,128,256]{2,1,0:T(8,128)(2,1)S(1)} async-done(((bf16[16,128,256]{2,1,0:T(8,128)(2,1)}), bf16[16,128,256]{2,1,0:T(8,128)(2,1)S(1)}, u32[]{:S(2)}, u32[]{:S(2)}) %all-to-all-start.1) | async-done | bytes 1048608 | tf_op jit(solution)/shard_map/all_to_all | solution.py:44
  59.8 1.5 fusion.23
  61.5 1.5 convolution_convert_fusion.3
  63.1 2.0 fusion.29
  66.3 3.3 %fusion.18 = bf16[2048,256]{1,0:T(8,128)(2,1)} fusion(bf16[1024,256]{1,0:T(8,128)(2,1)S(1)} %reshape.44, s32[2048]{0:T(1024)S(1)} %bitcast.22), kind=kOutput, calls=%fused_computation.19 | convolution fusion | flops 1076363264 | bytes 1581056 | tf_op jit(solution)/shard_map/dot_general | solution.py:15
  69.6 5.8 %all-to-all-start.2 = ((bf16[16,128,256]{2,1,0:T(8,128)(2,1)}), bf16[16,128,256]{2,1,0:T(8,128)(2,1)S(1)}, u32[]{:S(2)}, u32[]{:S(2)}) async-start(bf16[16,128,256]{2,1,0:T(8,128)(2,1)} %bitcast.3), calls=%async_computation.3 | async-start | bytes 2097152 | tf_op jit(solution)/shard_map/all_to_all | solution.py:93
  76.2 23.0 %all-to-all-done.2 = bf16[16,128,256]{2,1,0:T(8,128)(2,1)S(1)} async-done(((bf16[16,128,256]{2,1,0:T(8,128)(2,1)}), bf16[16,128,256]{2,1,0:T(8,128)(2,1)S(1)}, u32[]{:S(2)}, u32[]{:S(2)}) %all-to-all-start.2) | async-done | bytes 1048608 | tf_op jit(solution)/shard_map/all_to_all | solution.py:93
  99.1 5.5 %fusion.20 = bf16[1024,256]{1,0:T(8,128)(2,1)} fusion(bf16[2048,256]{1,0:T(8,128)(2,1)S(1)} %bitcast.20, s32[2048]{0:T(1024)S(1)} %get-tuple-element.21, s32[2048]{0:T(1024)S(1)} %get-tuple-element.22, s32[2048]{0:T(1024)S(1)} %get-tuple-element.23, s32[2048]{0:T(1024)S(1)} %get-tuple-element.20), kind=kOutput, calls=%fused_computation.31 | convolution fusion | flops 1107558400 | bytes 1605632 | tf_op jit(solution)/shard_map/dot_general | solution.py:15
  105.2 1.5 pad_maximum_fusion
  106.7 17.0 %all-reduce.3.cloned.1.call-done = bf16[1024,256]{1,0:T(8,128)(2,1)} async-done(((bf16[1024,256]{1,0:T(8,128)(2,1)}), bf16[1024,256]{1,0:T(8,128)(2,1)}) %all-reduce.3.cloned.1.call-update) | async-done | bytes 524304 | tf_op jit(solution)/shard_map/psum | solution.py:99
  123.7 1.3 fusion.24
  125.7 2.1 fusion.26
  127.8 8.9 %reduce-scatter.2.cloned.1.call-done = bf16[1024,512]{0,1:T(8,128)(2,1)} async-done(((bf16[2048,512]{0,1:T(8,128)(2,1)}), bf16[1024,512]{0,1:T(8,128)(2,1)}) %reduce-scatter.2.cloned.1.call-update) | async-done | bytes 1048592 | tf_op jit(solution)/shard_map/reduce_scatter | solution.py:73
  136.7 100.9 %all-reduce.4 = f32[1024,512]{0,1:T(8,128)S(1)} all-reduce(bf16[1024,512]{0,1:T(8,128)(2,1)} %reduce-scatter.2.cloned.1.call-done), channel_id=1, replica_groups=mesh['table'=16,'narrow'=2] {'table'}, use_global_device_ids=true, to_apply=%region_2.0 | all-reduce | flops 524288 | bytes 3145728 | tf_op jit(solution)/shard_map/psum | solution.py:81
  238.2 1.3 copy.19
  239.5 1.3 copy.18
  (39 shorter events, 4.0 us)
Async XLA Ops:
  24.6 2.0 copy-start.2
  32.7 5.3 %copy-start.4 = (bf16[2048]{0:T(1024)(128)(2,1)S(1)}, bf16[2048]{0:T(1024)(128)(2,1)}, u32[]{:S(2)}) copy-start(bf16[2048]{0:T(1024)(128)(2,1)} %param.14) | copy-start | bytes 12292
  32.7 27.1 %copy-start.7 = (s32[16,128]{1,0:T(8,128)S(1)}, s32[16,128]{1,0:T(8,128)}, u32[]{:S(2)}) copy-start(s32[16,128]{1,0:T(8,128)} %param.17) | copy-start | bytes 24580
  32.7 27.1 %all-to-all-start.1 = ((bf16[16,128,256]{2,1,0:T(8,128)(2,1)}), bf16[16,128,256]{2,1,0:T(8,128)(2,1)S(1)}, u32[]{:S(2)}, u32[]{:S(2)}) async-start(bf16[16,128,256]{2,1,0:T(8,128)(2,1)} %bitcast.1), calls=%async_computation.1 | async-start | bytes 2097152 | tf_op jit(solution)/shard_map/all_to_all | solution.py:44
  36.5 25.0 %all-gather.3.cloned.1.call-start = ((), (), s32[]{:S(2)}) async-start(), calls=%async_computation.4 | async-start | bytes 1572864 | tf_op jit(solution)/shard_map/all_gather | solution.py:55
  37.2 25.9 %all-gather.5.cloned.1.call-start = ((), (), s32[]{:S(2)}) async-start(), calls=%async_computation.5 | async-start | bytes 1572864 | tf_op jit(solution)/shard_map/all_gather | solution.py:56
  61.2 1.9 copy-start.3
  61.5 3.6 %copy-start.8 = (f32[128]{0:T(128)S(1)}, f32[128]{0:T(128)}, u32[]{:S(2)}) copy-start(f32[128]{0:T(128)} %param.15) | copy-start | bytes 1540
  63.1 2.4 copy-start
  63.1 2.0 copy-start.1
  65.1 0.9 copy-start.6
  69.6 29.5 %all-to-all-start.2 = ((bf16[16,128,256]{2,1,0:T(8,128)(2,1)}), bf16[16,128,256]{2,1,0:T(8,128)(2,1)S(1)}, u32[]{:S(2)}, u32[]{:S(2)}) async-start(bf16[16,128,256]{2,1,0:T(8,128)(2,1)} %bitcast.3), calls=%async_computation.3 | async-start | bytes 2097152 | tf_op jit(solution)/shard_map/all_to_all | solution.py:93
  75.4 48.3 %all-reduce.3.cloned.1.call-start = ((), (), s32[]{:S(2)}) async-start(), calls=%async_computation.7 | async-start | bytes 1048576 | tf_op jit(solution)/shard_map/psum | solution.py:99
  104.6 32.1 %reduce-scatter.2.cloned.1.call-start = ((), (), s32[]{:S(2)}) async-start(), calls=%async_computation.6 | async-start | bytes 3145728 | tf_op jit(solution)/shard_map/reduce_scatter | solution.py:73
  106.7 18.3 %copy-start.5 = (f32[1024]{0:T(1024)S(1)}, f32[1024]{0:T(1024)}, u32[]{:S(2)}) copy-start(f32[1024]{0:T(1024)} %param.10) | copy-start | bytes 12292
Sparse Core Ops, SparseCore 0:
  38.9 10.2 all-gather.2
  50.7 10.1 all-gather.4
  104.8 18.9 all-reduce.2
  125.9 10.7 reduce-scatter.1
where the time goes:
time: 248 us; the launch traced here: 247 us
  blocking collectives  116 us (47%)
  waiting for transfers between devices  72.1 us (29%)
  matrix products  21.7 us (9%)
  between operations  14 us (6%)
  starting transfers between devices  9.95 us (4%)
  local copies, waits for them, and re-layouts  7.88 us (3%)
  other arithmetic  5.22 us (2%)
    psum x1, blocking collectives, local(): grand_total = lax.psum(narrow_sum, 'table')  101 us
    all_to_all x1, waiting for transfers between devices, local(): lax.all_to_all(slot_grads, 'table', split_axis=0, concat_axis=0, tiled=True)  23 us
    all_to_all x1, waiting for transfers between devices, local(): lax.all_to_all(pool_out, 'table', split_axis=0, concat_axis=0, tiled=True)  21.7 us
    psum x1, waiting for transfers between devices, local(): lax.psum(local_grad.astype(jnp.bfloat16), 'narrow').astype(jnp.float32)  17 us
    all_to_all x1, blocking collectives, local(): lax.all_to_all(bag_rows, 'table', split_axis=0, concat_axis=0, tiled=True)  15.5 us
    dot_general x4, matrix products, transposed_dot(): lax.dot_general(left, right, (((0,), (0,)), ((), ())), preferred_element_...  9.82 us
    reduce_scatter x1, waiting for transfers between devices, local(): lax.psum_scatter(jnp.concatenate([transposed_dot(pooled_feats, dhidden),...  8.95 us
    dot_general x1, matrix products, local(): pool_sums = jnp.dot(counts, table_rows, preferred_element_type=jnp.float32)  6.07 us
  transfers between devices with their start and end apart: 6, of which 4 were waited for; matrix products, arithmetic and copies ran while one was open for 4% of the time, Pallas kernels for 0%

commit v1 on v0

--- a/solution.py
+++ b/solution.py
@@ -78,7 +78,11 @@
         scatter_dimension=0,
         tiled=True,
     ).astype(jnp.float32)
-    grand_total = lax.psum(narrow_sum, "table")
+    grand_total = narrow_sum
+    for hop in (1, 2, 4, 8):
+        grand_total = grand_total + lax.ppermute(
+            grand_total, "table", [(dev, dev ^ hop) for dev in range(16)]
+        )
     batch_all = samples * tables * narrows
     grand_total = grand_total * (1.0 / math.sqrt(batch_all))
     rank_size = factor_down.shape[1]

time: 248 us -> 339 us (1.37)
  waiting for transfers between devices: 72.1 us -> 249 us
  blocking collectives: 116 us -> 15.5 us
  other arithmetic: 5.22 us -> 12.1 us
  starting transfers between devices: 9.95 us -> 15.3 us
    ppermute x0 -> x4, waiting for transfers between devices: none -> 193 us  [local(): lax.ppermute(grand_total, 'table', [(dev, dev ^ hop) for dev in range(16)])]
    psum x1 -> x0, blocking collectives: 101 us -> none  [local(): grand_total = lax.psum(narrow_sum, 'table')]
    all_to_all x1, waiting for transfers between devices: 23 us -> 5.97 us  [local(): lax.all_to_all(slot_grads, 'table', split_axis=0, concat_axis=0, tiled=True)]
    ppermute x0 -> x4, starting transfers between devices: none -> 5.51 us  [local(): lax.ppermute(grand_total, 'table', [(dev, dev ^ hop) for dev in range(16)])]
    add x0 -> x3, other arithmetic: none -> 3.44 us  [local(): grand_total + lax.ppermute(grand_total, 'table', [(dev, dev ^ hop) for de...]
  transfers between devices with their start and end apart: 6 -> 10, of which waited for: 4 -> 8; matrix products, arithmetic and copies ran while one was open for 4% -> 7% of each run, Pallas kernels for 0% -> 0%
where the time goes in v1:
time: 339 us; the launch traced here: 338 us
  waiting for transfers between devices  249 us (73%)
  matrix products  23.7 us (7%)
  blocking collectives  15.5 us (5%)
  starting transfers between devices  15.3 us (5%)
  between operations  14 us (4%)
  other arithmetic  12.1 us (4%)
  local copies, waits for them, and re-layouts  8.82 us (3%)
    ppermute x4, waiting for transfers between devices, local(): lax.ppermute(grand_total, 'table', [(dev, dev ^ hop) for dev in range(16)])  193 us
    all_to_all x1, waiting for transfers between devices, local(): lax.all_to_all(pool_out, 'table', split_axis=0, concat_axis=0, tiled=True)  21.7 us
    psum x1, waiting for transfers between devices, local(): lax.psum(local_grad.astype(jnp.bfloat16), 'narrow').astype(jnp.float32)  17 us
    all_to_all x1, blocking collectives, local(): lax.all_to_all(bag_rows, 'table', split_axis=0, concat_axis=0, tiled=True)  15.5 us
    dot_general x4, matrix products, transposed_dot(): lax.dot_general(left, right, (((0,), (0,)), ((), ())), preferred_element_...  11.1 us
    reduce_scatter x1, waiting for transfers between devices, local(): lax.psum_scatter(jnp.concatenate([transposed_dot(pooled_feats, dhidden),...  9.97 us
  transfers between devices with their start and end apart: 10, of which 8 were waited for; matrix products, arithmetic and copies ran while one was open for 7% of the time, Pallas kernels for 0%

profile of v1, /device:TPU:0, one launch (start us, length us, event | category | flops | bytes accessed | tf_op | source)
XLA Modules:
  0.0 338.1 jit_solution(13713627515984569368)
XLA Ops:
  8.0 15.5 %all_to_all.19 = s32[16,1,512]{2,1,0:T(1,128)S(1)} all-to-all(s32[16,1,512]{2,1,0:T(1,128)S(1)} %all_to_all.12), channel_id=1, replica_groups=mesh['table'=16,'narrow'=2] {'table'}, dimensions={0} | all-to-all | bytes 65536 | tf_op jit(solution)/shard_map/all_to_all | solution.py:36
  24.6 2.0 slice_reduce_fusion.3
  26.6 6.1 %fusion.15 = bf16[2048,256]{1,0:T(8,128)(2,1)} fusion(bf16[1024,256]{1,0:T(8,128)(2,1)S(1)} %copy-done.4, s32[2048]{0:T(1024)S(1)} %get-tuple-element.21, s32[2048]{0:T(1024)S(1)} %get-tuple-element.22, s32[2048]{0:T(1024)S(1)} %get-tuple-element.23, s32[2048]{0:T(1024)S(1)} %get-tuple-element.20), kind=kOutput, calls=%fused_computation.18 | convolution fusion | flops 1107820544 | bytes 1605632 | tf_op jit(solution)/shard_map/dot_general | solution.py:42
  32.7 3.8 %all-to-all-start.1 = ((bf16[16,128,256]{2,1,0:T(8,128)(2,1)}), bf16[16,128,256]{2,1,0:T(8,128)(2,1)S(1)}, u32[]{:S(2)}, u32[]{:S(2)}) async-start(bf16[16,128,256]{2,1,0:T(8,128)(2,1)} %bitcast.1), calls=%async_computation.1 | async-start | bytes 2097152 | tf_op jit(solution)/shard_map/all_to_all | solution.py:44
  38.0 21.7 %all-to-all-done.1 = bf16[16,128,256]{2,1,0:T(8,128)(2,1)S(1)} async-done(((bf16[16,128,256]{2,1,0:T(8,128)(2,1)}), bf16[16,128,256]{2,1,0:T(8,128)(2,1)S(1)}, u32[]{:S(2)}, u32[]{:S(2)}) %all-to-all-start.1) | async-done | bytes 1048608 | tf_op jit(solution)/shard_map/all_to_all | solution.py:44
  63.1 1.9 fusion.29
  66.4 1.6 pad_maximum_fusion
  68.1 10.0 %reduce-scatter.2.cloned.1.call-done = bf16[1024,512]{0,1:T(8,128)(2,1)} async-done(((bf16[2048,512]{0,1:T(8,128)(2,1)}), bf16[1024,512]{0,1:T(8,128)(2,1)}) %reduce-scatter.2.cloned.1.call-update) | async-done | bytes 1048592 | tf_op jit(solution)/shard_map/reduce_scatter | solution.py:73
  78.0 1.5 convert_element_type.67
  79.6 1.8 collective-permute-start
  81.4 46.1 %collective-permute-done = f32[1024,512]{0,1:T(8,128)S(1)} collective-permute-done((f32[1024,512]{0,1:T(8,128)S(1)}, f32[1024,512]{0,1:T(8,128)S(1)}, u32[]{:S(2)}, u32[]{:S(2)}) %collective-permute-start) | collective-permute-done | bytes 2097184 | tf_op jit(solution)/shard_map/ppermute | solution.py:83
  127.9 1.8 collective-permute-start.1
  129.7 45.3 %collective-permute-done.1 = f32[1024,512]{0,1:T(8,128)S(1)} collective-permute-done((f32[1024,512]{0,1:T(8,128)S(1)}, f32[1024,512]{0,1:T(8,128)S(1)}, u32[]{:S(2)}, u32[]{:S(2)}) %collective-permute-start.1) | collective-permute-done | bytes 2097184 | tf_op jit(solution)/shard_map/ppermute | solution.py:83
  175.4 1.8 collective-permute-start.2
  179.8 3.3 fusion.18
  183.2 5.6 %all-to-all-start.2 = ((bf16[16,128,256]{2,1,0:T(8,128)(2,1)}), bf16[16,128,256]{2,1,0:T(8,128)(2,1)}, u32[]{:S(2)}, u32[]{:S(2)}) async-start(bf16[16,128,256]{2,1,0:T(8,128)(2,1)} %bitcast.3), calls=%async_computation.3 | async-start | bytes 2097152 | tf_op jit(solution)/shard_map/all_to_all | solution.py:97
  189.0 46.3 %collective-permute-done.2 = f32[1024,512]{0,1:T(8,128)} collective-permute-done((f32[1024,512]{0,1:T(8,128)S(1)}, f32[1024,512]{0,1:T(8,128)}, u32[]{:S(2)}, u32[]{:S(2)}) %collective-permute-start.2) | collective-permute-done | bytes 2097184 | tf_op jit(solution)/shard_map/ppermute | solution.py:83
  235.3 2.6 add.69
  238.0 6.0 %all-to-all-done.2 = bf16[16,128,256]{2,1,0:T(8,128)(2,1)} async-done(((bf16[16,128,256]{2,1,0:T(8,128)(2,1)}), bf16[16,128,256]{2,1,0:T(8,128)(2,1)}, u32[]{:S(2)}, u32[]{:S(2)}) %all-to-all-start.2) | async-done | bytes 1048608 | tf_op jit(solution)/shard_map/all_to_all | solution.py:97
  244.0 6.8 %fusion.20 = bf16[1024,256]{1,0:T(8,128)(2,1)} fusion(bf16[2048,256]{1,0:T(8,128)(2,1)} %bitcast.4, s32[2048]{0:T(1024)S(1)} %get-tuple-element.21, s32[2048]{0:T(1024)S(1)} %get-tuple-element.22, s32[2048]{0:T(1024)S(1)} %get-tuple-element.23, s32[2048]{0:T(1024)S(1)} %get-tuple-element.20), kind=kOutput, calls=%fused_computation.32 | convolution fusion | flops 1107558400 | bytes 1605632 | tf_op jit(solution)/shard_map/dot_general | solution.py:15
  250.8 17.0 %all-reduce.2.cloned.1.call-done = bf16[1024,256]{1,0:T(8,128)(2,1)} async-done(((bf16[1024,256]{1,0:T(8,128)(2,1)}), bf16[1024,256]{1,0:T(8,128)(2,1)}) %all-reduce.2.cloned.1.call-update) | async-done | bytes 524304 | tf_op jit(solution)/shard_map/psum | solution.py:103
  269.8 2.1 fusion.26
  271.9 54.9 %collective-permute-done.3 = f32[1024,512]{0,1:T(8,128)} collective-permute-done((f32[1024,512]{0,1:T(8,128)S(1)}, f32[1024,512]{0,1:T(8,128)}, u32[]{:S(2)}, u32[]{:S(2)}) %collective-permute-start.3) | collective-permute-done | bytes 2097184 | tf_op jit(solution)/shard_map/ppermute | solution.py:83
  326.8 2.0 add_multiply_fusion
  (56 shorter events, 16.5 us)
Async XLA Ops:
  24.6 2.0 copy-start.4
  32.7 5.3 %copy-start.7 = (bf16[2048]{0:T(1024)(128)(2,1)S(1)}, bf16[2048]{0:T(1024)(128)(2,1)}, u32[]{:S(2)}) copy-start(bf16[2048]{0:T(1024)(128)(2,1)} %param.14) | copy-start | bytes 12292
  32.7 27.1 %copy-start.10 = (s32[16,128]{1,0:T(8,128)S(1)}, s32[16,128]{1,0:T(8,128)}, u32[]{:S(2)}) copy-start(s32[16,128]{1,0:T(8,128)} %param.17) | copy-start | bytes 24580
  32.7 27.1 %all-to-all-start.1 = ((bf16[16,128,256]{2,1,0:T(8,128)(2,1)}), bf16[16,128,256]{2,1,0:T(8,128)(2,1)S(1)}, u32[]{:S(2)}, u32[]{:S(2)}) async-start(bf16[16,128,256]{2,1,0:T(8,128)(2,1)} %bitcast.1), calls=%async_computation.1 | async-start | bytes 2097152 | tf_op jit(solution)/shard_map/all_to_all | solution.py:44
  36.5 25.0 %all-gather.3.cloned.1.call-start = ((), (), s32[]{:S(2)}) async-start(), calls=%async_computation.4 | async-start | bytes 1572864 | tf_op jit(solution)/shard_map/all_gather | solution.py:55
  37.2 25.8 %all-gather.5.cloned.1.call-start = ((), (), s32[]{:S(2)}) async-start(), calls=%async_computation.5 | async-start | bytes 1572864 | tf_op jit(solution)/shard_map/all_gather | solution.py:56
  38.0 40.1 %reduce-scatter.2.cloned.1.call-start = ((), (), s32[]{:S(2)}) async-start(), calls=%async_computation.6 | async-start | bytes 3145728 | tf_op jit(solution)/shard_map/reduce_scatter | solution.py:73
  61.2 1.9 copy-start.6
  61.5 3.6 %copy-start.11 = (f32[128]{0:T(128)S(1)}, f32[128]{0:T(128)}, u32[]{:S(2)}) copy-start(f32[128]{0:T(128)} %param.15) | copy-start | bytes 1540
  63.1 2.5 copy-start.3
  65.0 1.4 copy-start.9
  78.0 49.4 %copy-start.1 = (bf16[1024,512]{0,1:T(8,128)(2,1)S(1)}, bf16[1024,512]{0,1:T(8,128)(2,1)}, u32[]{:S(2)}) copy-start(bf16[1024,512]{0,1:T(8,128)(2,1)} %reduce-scatter.2.cloned.1.call-done) | copy-start | bytes 3145732
  79.6 47.9 %collective-permute-start = (f32[1024,512]{0,1:T(8,128)S(1)}, f32[1024,512]{0,1:T(8,128)S(1)}, u32[]{:S(2)}, u32[]{:S(2)}) collective-permute-start(f32[1024,512]{0,1:T(8,128)S(1)} %convert_element_type.67), channel_id=1, source_target_pairs={{0,2},{2,0},{4,6},{6,4},{8,10},{10,8},{12,14},{14,12},{16,18},{18,... | collective-permute-start | bytes 6291464 | tf_op jit(solution)/shard_map/ppermute | solution.py:83
  127.9 49.3 %copy-start.2 = (bf16[2048,256]{1,0:T(8,128)(2,1)S(1)}, bf16[2048,256]{1,0:T(8,128)(2,1)}, u32[]{:S(2)}) copy-start(bf16[2048,256]{1,0:T(8,128)(2,1)} %all-gather.3.cloned.1.call-done) | copy-start | bytes 3145732
  127.9 47.1 %collective-permute-start.1 = (f32[1024,512]{0,1:T(8,128)S(1)}, f32[1024,512]{0,1:T(8,128)S(1)}, u32[]{:S(2)}, u32[]{:S(2)}) collective-permute-start(f32[1024,512]{0,1:T(8,128)S(1)} %convert_add_fusion), channel_id=1, source_target_pairs={{0,4},{2,6},{4,0},{6,2},{8,12},{10,14},{12,8},{14,10},{16,20},{18,... | collective-permute-start | bytes 6291464 | tf_op jit(solution)/shard_map/ppermute | solution.py:83
  175.4 7.8 %copy-start = (f32[1024,512]{0,1:T(8,128)}, f32[1024,512]{0,1:T(8,128)S(1)}, u32[]{:S(2)}) copy-start(f32[1024,512]{0,1:T(8,128)S(1)} %add.68) | copy-start | bytes 6291460
  175.4 59.9 %collective-permute-start.2 = (f32[1024,512]{0,1:T(8,128)S(1)}, f32[1024,512]{0,1:T(8,128)}, u32[]{:S(2)}, u32[]{:S(2)}) collective-permute-start(f32[1024,512]{0,1:T(8,128)S(1)} %add.68), channel_id=1, source_target_pairs={{0,8},{2,10},{4,12},{6,14},{8,0},{10,2},{12,4},{14,6},{16,24},{18,... | collective-permute-start | bytes 6291464 | tf_op jit(solution)/shard_map/ppermute | solution.py:83
  183.2 60.8 %all-to-all-start.2 = ((bf16[16,128,256]{2,1,0:T(8,128)(2,1)}), bf16[16,128,256]{2,1,0:T(8,128)(2,1)}, u32[]{:S(2)}, u32[]{:S(2)}) async-start(bf16[16,128,256]{2,1,0:T(8,128)(2,1)} %bitcast.3), calls=%async_computation.3 | async-start | bytes 2097152 | tf_op jit(solution)/shard_map/all_to_all | solution.py:97
  188.8 79.0 %all-reduce.2.cloned.1.call-start = ((), (), s32[]{:S(2)}) async-start(), calls=%async_computation.7 | async-start | bytes 1048576 | tf_op jit(solution)/shard_map/psum | solution.py:103
  238.0 88.8 %collective-permute-start.3 = (f32[1024,512]{0,1:T(8,128)S(1)}, f32[1024,512]{0,1:T(8,128)}, u32[]{:S(2)}, u32[]{:S(2)}) collective-permute-start(f32[1024,512]{0,1:T(8,128)S(1)} %add.69), channel_id=1, source_target_pairs={{0,16},{2,18},{4,20},{6,22},{8,24},{10,26},{12,28},{14,30},{16,0},... | collective-permute-start | bytes 6291464 | tf_op jit(solution)/shard_map/ppermute | solution.py:83
  244.0 25.1 %copy-start.8 = (f32[1024]{0:T(1024)S(1)}, f32[1024]{0:T(1024)}, u32[]{:S(2)}) copy-start(f32[1024]{0:T(1024)} %param.10) | copy-start | bytes 12292
  244.0 25.7 %copy-start.5 = (bf16[1024,256]{1,0:T(8,128)(2,1)S(1)}, bf16[1024,256]{1,0:T(8,128)(2,1)}, u32[]{:S(2)}) copy-start(bf16[1024,256]{1,0:T(8,128)(2,1)} %param.9) | copy-start | bytes 1572868
Sparse Core Ops, SparseCore 0:
  38.9 10.2 all-gather.2
  50.7 10.1 all-gather.4
  68.2 9.8 reduce-scatter.1
  250.9 16.8 all-reduce.1
